TPU v7x, 32 devices: a whole 2x2x4 slice. The times are simulated.
32 devices in a mesh: space: 8 (over z, core), spec: 4 (over y, x).
Axes of the slice: x: 2, y: 2, z: 4, core: 2. Of those that a mesh axis runs over, the one named last changes fastest.
Arguments:
- action: float32 [16, 24, 64, 512], P('spec', None, 'space'), may hold values from 0.1 to 1
- currents: float32 [2, 128, 1024], P(None, 'space', 'spec'), may hold values from -1.2 to 1.2
- wet: int32 [128, 1024], P('space', 'spec'), may hold values 0 or 1
- courant: float32 [16], replicated, may hold values from 0.1 to 0.35
- energy: float32 [16], replicated, may hold values from 0.3 to 3
- src: int32 [96, 512, 4], P('space'), may hold values from 4096 to 29695, as said below
- weights: float32 [96, 512, 4], P('space'), as said below
Outputs:
- new_action: float32 [16, 24, 64, 512], P('spec', None, 'space')
- new_currents: float32 [2, 128, 1024], P(None, 'space', 'spec')
Inputs may be any that keep to these rules, and one draw needn't show every extreme that they name: `src`: row e of block s refers to ocean rows 2 (e - 2) + 8 + j + a of the pair of ocean row blocks s and s + 1 (j 0 or 1 per wave cell, a the corner's row bit) and columns (2 x + i + b) mod 1024; the four corners of a cell are distinct; the two outer rows on each side of a block's lists refer to the same ocean cells, with the same weights, as the lists of the same wave rows in the neighbouring blocks. Positive; the 4 weights of a wave cell sum to one; rows that describe the same wave row are equal.
All inputs are finite; a program needn't handle non-finite values. No bound on the sum of `wet` on one device may be relied on, other than what follows from the above.
Results may differ from a plain program's by a relative error of at most 0.00009.
Values sent between devices are 32-bit elements; how exact they have to be, the bound alone decides.
No kernel may reach another device: no remote copies, remote signals or barrier semaphores. Data moves between devices by JAX's collectives and lax.ppermute only.
A program may use at most 128 MiB of HBM per device.

v0:
```python
import math
import jax
import jax.numpy as jnp
from jax import lax
from jax.sharding import PartitionSpec as P

drift_factor = 0.2
refract_factor = 1.5
damping = 0.95
force_gain = 0.5


def from_behind(block, axis, distance):
    devices = range(lax.axis_size(axis))
    route = [((i - distance) % len(devices), i) for i in devices]
    return lax.ppermute(block, axis, route)


def with_halo(cells, sides, width):
    for axis, dim in sides:
        count = lax.axis_size(axis)
        head = lax.slice_in_dim(cells, 0, width, axis=dim)
        tail = lax.slice_in_dim(cells, cells.shape[dim] - width, cells.shape[dim], axis=dim)
        cells = jnp.concatenate(
            [
                lax.ppermute(tail, axis, [(i, (i + 1) % count) for i in range(count)]),
                cells,
                lax.ppermute(head, axis, [((i + 1) % count, i) for i in range(count)]),
            ],
            axis=dim,
        )
    return cells


def advance(extended, speeds, flow, cosine, sine):
    east, north = (flow[0], flow[1])
    east_mid, north_mid = (east[1:-1], north[1:-1])
    grad_east_x = (jnp.roll(east_mid, -1, 1) - jnp.roll(east_mid, 1, 1)) * 0.5
    grad_north_x = (jnp.roll(north_mid, -1, 1) - jnp.roll(north_mid, 1, 1)) * 0.5
    grad_east_y = (east[2:] - east[:-2]) * 0.5
    grad_north_y = (north[2:] - north[:-2]) * 0.5
    cos3, sin3 = (cosine[:, None, None], sine[:, None, None])
    turn = refract_factor * (
        sin3 * cos3 * (grad_east_x - grad_north_y)[None]
        + sin3 * sin3 * grad_east_y[None]
        - cos3 * cos3 * grad_north_x[None]
    )
    speed_four = speeds[:, None, None, None]
    centre = extended[:, :, 1:-1]
    speed_x = speed_four * cos3[None] + drift_factor * east_mid[None, None]
    face_x = jnp.maximum(speed_x, 0.0) * centre + jnp.minimum(
        jnp.roll(speed_x, -1, 3), 0.0
    ) * jnp.roll(centre, -1, 3)
    speed_y = speed_four * sin3[None] + drift_factor * north[None, None]
    face_y = (
        jnp.maximum(speed_y[:, :, :-1], 0.0) * extended[:, :, :-1]
        + jnp.minimum(speed_y[:, :, 1:], 0.0) * extended[:, :, 1:]
    )
    face_turn = jnp.maximum(turn, 0.0)[None] * centre + jnp.minimum(jnp.roll(turn, -1, 0), 0.0)[
        None
    ] * jnp.roll(centre, -1, 1)
    return (
        centre
        - (face_x - jnp.roll(face_x, 1, 3))
        - (face_y[:, :, 1:] - face_y[:, :, :-1])
        - (face_turn - jnp.roll(face_turn, 1, 1))
    )


def stencil_tables(src, weights, ocean_cols, wave_rows):
    list_rows = src.shape[0]
    columns = src.shape[1]
    base_row = 2 * (jnp.arange(list_rows, dtype=jnp.int32) - 2) + wave_rows
    row_offset = src // ocean_cols - base_row[:, None, None]
    col_offset = (
        src % ocean_cols - 2 * jnp.arange(columns, dtype=jnp.int32)[None, :, None]
    ) % ocean_cols
    tables = []
    for step_row in range(3):
        for step_col in range(3):
            hit = jnp.logical_and(row_offset == step_row, col_offset == step_col)
            tables.append(jnp.sum(jnp.where(hit, weights, 0.0), axis=-1))
    return tables


def per_device(action, currents, wet, courant, energy, src, weights):
    wet_float = wet.astype(jnp.float32)
    masked = currents * wet_float[None]
    row_local = lax.all_gather(masked, "spec", axis=2, tiled=True)
    row_next = from_behind(row_local, "space", -1)
    ocean_rows = row_local.shape[1]
    ocean_cols = row_local.shape[2]
    wave_rows = action.shape[2]
    columns = src.shape[1]
    list_rows = src.shape[0]
    paired = jnp.concatenate([row_local, row_next], axis=1)
    tables = stencil_tables(src, weights, ocean_cols, wave_rows)
    first_row = wave_rows - 4
    window = paired[:, first_row : first_row + 2 * (list_rows + 1)].reshape(
        2, list_rows + 1, 2, columns, 2
    )
    drift = jnp.zeros((2, list_rows, columns), jnp.float32)
    for step_row in range(3):
        for step_col in range(3):
            lifted = window[
                :, step_row // 2 : step_row // 2 + list_rows, step_row % 2, :, step_col % 2
            ]
            if step_col == 2:
                lifted = jnp.roll(lifted, -1, 2)
            drift = drift + tables[3 * step_row + step_col][None] * lifted
    count_freq = action.shape[0]
    directions = action.shape[1]
    total_freq = count_freq * lax.axis_size("spec")
    start = lax.axis_index("spec") * count_freq
    freq_index = start + jnp.arange(count_freq, dtype=jnp.int32)
    speed_local = lax.dynamic_slice_in_dim(courant, start, count_freq)
    energy_local = lax.dynamic_slice_in_dim(energy, start, count_freq)
    angles = 2.0 * math.pi * (jnp.arange(directions, dtype=jnp.float32) + 0.5) / directions
    cosine, sine = (jnp.cos(angles), jnp.sin(angles))
    field = action
    for substep in range(2):
        extended = with_halo(field, (("space", 2),), 1)
        field = advance(extended, speed_local, drift[:, 1:-1], cosine, sine)
    ratio = 0.5 + 0.5 * freq_index.astype(jnp.float32) / (total_freq - 1)
    amplitude = energy_local / math.sqrt(directions * total_freq)
    coef = jnp.stack(
        [
            amplitude[:, None] * (ratio[:, None] * (cosine * cosine)[None] + ratio[:, None] - 0.5),
            amplitude[:, None] * (ratio[:, None] * (sine * sine)[None] + ratio[:, None] - 0.5),
            amplitude[:, None] * ratio[:, None] * (sine * cosine)[None],
        ]
    )
    stress = jnp.einsum("kfd,fdrx->krx", coef, field, precision=lax.Precision.HIGHEST)
    stress = lax.psum(stress, "spec")
    rimmed = with_halo(stress, (("space", 1),), 1)
    middle_stress = rimmed[:, 1:-1]
    grad_x = (jnp.roll(middle_stress, -1, 2) - jnp.roll(middle_stress, 1, 2)) * 0.5
    grad_y = (rimmed[:, 2:] - rimmed[:, :-2]) * 0.5
    force = jnp.stack([-(grad_x[0] + grad_y[2]), -(grad_x[2] + grad_y[1])])
    grid = jnp.zeros((2, wave_rows + 1, 2, columns, 2), jnp.float32)
    for step_row in range(3):
        for step_col in range(3):
            placed = tables[3 * step_row + step_col][2 : 2 + wave_rows][None] * force
            if step_col == 2:
                placed = jnp.roll(placed, 1, 2)
            grid = grid.at[
                :, step_row // 2 : step_row // 2 + wave_rows, step_row % 2, :, step_col % 2
            ].add(placed)
    flat_grid = grid.reshape(2, 2 * (wave_rows + 1), ocean_cols)
    below_pad = 2 * ocean_rows - wave_rows - 2 * (wave_rows + 1)
    pair_force = jnp.pad(flat_grid, ((0, 0), (wave_rows, below_pad), (0, 0)))
    width = currents.shape[2]
    share = lax.dynamic_slice_in_dim(pair_force, lax.axis_index("spec") * width, width, 2)
    lower = share[:, :ocean_rows]
    upper = share[:, ocean_rows:]
    below = from_behind(upper, "space", 1)
    pushed = lower + below
    updated = wet_float[None] * (damping * currents + force_gain * pushed)
    return (field, updated)


def solution(mesh):
    in_specs = (
        P("spec", None, "space", None),
        P(None, "space", "spec"),
        P("space", "spec"),
        P(),
        P(),
        P("space", None, None),
        P("space", None, None),
    )
    out_specs = (P("spec", None, "space", None), P(None, "space", "spec"))
    return jax.shard_map(
        per_device, mesh=mesh, in_specs=in_specs, out_specs=out_specs, check_vma=False
    )
```

profile of v0, /device:TPU:0, one launch (start us, length us, event | category | flops | bytes accessed | tf_op | source)
XLA Modules:
  0.0 138.4 jit_solution(14236402526247451844)
XLA Ops:
  1.4 0.8 copy_multiply_fusion
  2.1 9.9 %all_gather.3 = f32[2,16,1024]{2,0,1:T(2,128)S(1)} all-gather(f32[2,16,256]{2,0,1:T(2,128)S(1)} %copy_multiply_fusion), channel_id=1, replica_groups=mesh['space'=8,'spec'=4] {'spec'}, dimensions={2}, use_global_device_ids=true | all-gather | bytes 163840 | tf_op jit(solution)/shard_map/all_gather | solution.py:89
  12.1 1.1 collective-permute-start
  13.2 2.3 %copy.134 = f32[4,24,8,512]{3,1,2,0:T(8,128)S(1)} copy(f32[4,24,8,512]{3,2,1,0:T(8,128)} %param.25) | data formatting | bytes 3145728 | tf_op args[0]
  15.5 0.9 fusion.50
  16.4 3.5 %collective-permute-start.2 = (f32[4,24,1,512]{3,1,2,0:T(8,128)}, f32[4,24,1,512]{3,1,2,0:T(8,128)}, u32[]{:S(2)}, u32[]{:S(2)}) collective-permute-start(f32[4,24,1,512]{3,1,2,0:T(8,128)} %get-tuple-element.155), channel_id=1, source_target_pairs={{4,0},{8,4},{12,8},{16,12},{20,16},{24,20},{28,24},{0,28},{5,1},{9... | collective-permute-start | bytes 589832 | tf_op jit(solution)/shard_map/ppermute | solution.py:28
  23.9 1.4 %slice.802 = f32[4,23,8,512]{3,1,2,0:T(8,128)} slice(f32[4,24,8,512]{3,1,2,0:T(8,128)S(1)} %copy.134), slice={[0:4], [1:24], [0:8], [0:512]} | slice | bytes 3014656 | tf_op jit(solution)/shard_map/jit(_roll_static)/slice | solution.py:61
  31.6 1.0 pad_maximum_fusion
  32.6 19.8 %reshape.996 = f32[2,13,2,512,2]{4,3,0,2,1:T(8,128)} reshape(f32[2,26,1024]{2,0,1:T(2,128)S(1)} %pad_maximum_fusion) | data formatting | bytes 425984 | tf_op jit(solution)/shard_map/reshape | solution.py:99
  52.4 21.7 %slice_reduce_fusion.4 = (f32[2,12,512]{2,0,1:T(2,128)S(1)}, f32[2,12,512]{2,0,1:T(2,128)S(1)}, f32[2,12,512]{2,0,1:T(2,128)S(1)}, f32[2,12,512]{2,0,1:T(2,128)S...) fusion(f32[2,13,2,512,2]{4,3,0,2,1:T(8,128)} %reshape.996), kind=kLoop, calls=%fused_computation.4 | loop fusion | bytes 589824 | tf_op jit(solution)/shard_map/slice | solution.py:105
  78.0 1.9 %fusion.8 = (f32[4,24,8,512]{3,1,2,0:T(8,128)S(1)}, f32[4,24,8,512]{3,1,2,0:T(8,128)S(1)}) fusion(f32[4,1,8,512]{3,1,2,0:T(1,128)S(1)} %copy.144, f32[4,23,8,512]{3,1,2,0:T(8,128)S(1)} %copy-done.3, f32[24,8,512]{2,0,1:T(8,128)S(1)} %maximum_minimum_fusion.1, f32[24,8,512]{2,0,1:T(8,128)S(1)} %get-tuple-element.171, f32[4,24,8,512]{3,2,1,0:T(8,128)S(1)} %copy-done.2, ...), kind=kLoop, calls=%fused_computation.26 | loop fusion | flops 4718592 | bytes 10240384 | tf_op jit(solution)/shard_map/add | solution.py:59
  81.3 1.5 %fusion = f32[4,24,9,512]{3,1,2,0:T(8,128)S(1)} fusion(f32[4,24,8,512]{3,1,2,0:T(8,128)S(1)} %copy-done.1, f32[4,24,1,512]{3,1,2,0:T(8,128)} %collective-permute-done.1, f32[4,24,1,512]{3,1,2,0:T(8,128)} %collective-permute-done.2, f32[4,24,10,512]{3,1,2,0:T(8,128)S(1)} %broadcast_add_fusion), kind=kLoop, calls=%fused_computation.9 | loop fusion | flops 3096576 | bytes 7274496 | tf_op jit(solution)/shard_map/add | solution.py:56
  82.9 2.4 %fusion.5 = f32[4,24,8,512]{3,1,2,0:T(8,128)S(1)} fusion(f32[4,24,9,512]{3,1,2,0:T(8,128)S(1)} %fusion, f32[4,24,8,512]{3,1,2,0:T(8,128)S(1)} %get-tuple-element.154, f32[4,24,8,511]{3,1,2,0:T(8,128)S(1)} %bitcast.61, f32[4,24,8,1]{3,1,2,0:T(8,128)S(1)} %slice.778, f32[4,24,8,512]{3,1,2,0:T(8,128)S(1)} %get-tuple-element.153, ...), kind=kLoop, calls=%fused_computation.19 | loop fusion | flops 3145728 | bytes 12582912 | tf_op jit(solution)/shard_map/sub | solution.py:63
  86.2 3.5 %collective-permute-start.4 = (f32[4,24,1,512]{3,1,2,0:T(8,128)S(1)}, f32[4,24,1,512]{3,1,2,0:T(8,128)S(1)}, u32[]{:S(2)}, u32[]{:S(2)}) collective-permute-start(f32[4,24,1,512]{3,1,2,0:T(8,128)S(1)} %get-tuple-element.151), channel_id=1, source_target_pairs={{4,0},{8,4},{12,8},{16,12},{20,16},{24,20},{28,24},{0,28},{5,1},{9... | collective-permute-start | bytes 589832 | tf_op jit(solution)/shard_map/ppermute | solution.py:28
  89.8 1.1 fusion.11
  91.1 3.4 %collective-permute-done.3 = f32[4,24,1,512]{3,1,2,0:T(8,128)S(1)} collective-permute-done((f32[4,24,1,512]{3,1,2,0:T(8,128)S(1)}, f32[4,24,1,512]{3,1,2,0:T(8,128)S(1)}, u32[]{:S(2)}, u32[]{:S(2)}) %collective-permute-start.3) | collective-permute-done | bytes 196640 | tf_op jit(solution)/shard_map/ppermute | solution.py:26
  95.0 1.4 %fusion.3 = f32[4,24,8,512]{3,1,2,0:T(8,128)S(1)} fusion(f32[4,24,9,512]{3,1,2,0:T(8,128)S(1)} %fusion.1, f32[4,24,8,512]{3,1,2,0:T(8,128)S(1)} %fusion.5, f32[4,24,8,512]{3,1,2,0:T(8,128)S(1)} %get-tuple-element.150, f32[4,24,8,511]{3,1,2,0:T(8,128)S(1)} %bitcast.60, f32[4,24,8,1]{3,1,2,0:T(8,128)S(1)} %slice.807, ...), kind=kLoop, calls=%fused_computation.16 | loop fusion | flops 3145728 | bytes 12582912 | tf_op jit(solution)/shard_map/sub | solution.py:63
  96.5 0.9 convolution_bitcast_fusion
  97.4 16.0 %psum.7 = f32[3,8,512]{2,0,1:T(4,128)S(1)} all-reduce(f32[3,8,512]{2,0,1:T(4,128)S(1)} %convolution_bitcast_fusion), channel_id=1, replica_groups=mesh['space'=8,'spec'=4] {'spec'}, use_global_device_ids=true, to_apply=%region_9.10 | all-reduce | flops 12288 | bytes 98304 | tf_op jit(solution)/shard_map/psum | solution.py:134
  115.1 3.6 %collective-permute-done.6 = f32[3,1,512]{2,0,1:T(4,128)S(1)} collective-permute-done((f32[3,1,512]{2,0,1:T(4,128)S(1)}, f32[3,1,512]{2,0,1:T(4,128)S(1)}, u32[]{:S(2)}, u32[]{:S(2)}) %collective-permute-start.6) | collective-permute-done | bytes 6176 | tf_op jit(solution)/shard_map/ppermute | solution.py:26
  119.8 5.0 %copy.148 = f32[2,9,2,512,2]{4,3,0,2,1:T(8,128)} copy(f32[2,9,2,512,2]{3,0,1,4,2:T(2,128)S(1)} %fusion.26) | data formatting | bytes 294912 | tf_op jit(solution)/shard_map/scatter-add | solution.py:148
  124.8 7.7 %reshape.1000 = f32[2,18,1024]{2,0,1:T(2,128)S(1)} reshape(f32[2,9,2,512,2]{4,3,0,2,1:T(8,128)} %copy.148) | data formatting | bytes 294912 | tf_op jit(solution)/shard_map/reshape | solution.py:149
  132.6 2.1 %copy.149 = f32[4,24,8,512]{3,2,1,0:T(8,128)} copy(f32[4,24,8,512]{3,1,2,0:T(8,128)S(1)} %fusion.3) | data formatting | bytes 3145728
  134.7 3.1 %collective-permute-done.7 = f32[2,16,256]{2,0,1:T(2,128)S(1)} collective-permute-done((f32[2,16,256]{2,0,1:T(2,128)S(1)}, f32[2,16,256]{2,0,1:T(2,128)S(1)}, u32[]{:S(2)}, u32[]{:S(2)}) %collective-permute-start.7) | collective-permute-done | bytes 32800 | tf_op jit(solution)/shard_map/ppermute | solution.py:16
  (168 shorter events, 20.9 us)
Async XLA Ops:
  12.1 8.1 %copy-start.30 = (f32[16]{0:T(128)S(1)}, f32[16]{0:T(128)}, u32[]{:S(2)}) copy-start(f32[16]{0:T(128)} %param.29) | copy-start | bytes 196
  12.1 8.2 %copy-start.11 = (s32[12,512,4]{1,2,0:T(4,128)S(1)}, s32[12,512,4]{1,2,0:T(4,128)}, u32[]{:S(2)}) copy-start(s32[12,512,4]{1,2,0:T(4,128)} %param.30) | copy-start | bytes 294916
  12.1 10.6 %copy-start.12 = (f32[12,512,4]{1,2,0:T(4,128)S(1)}, f32[12,512,4]{1,2,0:T(4,128)}, u32[]{:S(2)}) copy-start(f32[12,512,4]{1,2,0:T(4,128)} %param.31) | copy-start | bytes 294916
  12.1 19.5 %collective-permute-start = (f32[2,16,1024]{2,0,1:T(2,128)S(1)}, f32[2,16,1024]{2,0,1:T(2,128)}, u32[]{:S(2)}, u32[]{:S(2)}) collective-permute-start(f32[2,16,1024]{2,0,1:T(2,128)S(1)} %all_gather.3), channel_id=1, source_target_pairs={{4,0},{8,4},{12,8},{16,12},{20,16},{24,20},{28,24},{0,28},{5,1},{9... | collective-permute-start | bytes 393224 | tf_op jit(solution)/shard_map/ppermute | solution.py:16
  15.5 9.9 %copy-start = (f32[4,24,8,512]{3,1,2,0:T(8,128)}, f32[4,24,8,512]{3,1,2,0:T(8,128)S(1)}, u32[]{:S(2)}) copy-start(f32[4,24,8,512]{3,1,2,0:T(8,128)S(1)} %copy.134) | copy-start | bytes 4718596
  16.4 64.2 %collective-permute-start.1 = (f32[4,24,1,512]{3,1,2,0:T(8,128)}, f32[4,24,1,512]{3,1,2,0:T(8,128)}, u32[]{:S(2)}, u32[]{:S(2)}) collective-permute-start(f32[4,24,1,512]{3,1,2,0:T(8,128)} %get-tuple-element.156), channel_id=1, source_target_pairs={{0,4},{4,8},{8,12},{12,16},{16,20},{20,24},{24,28},{28,0},{1,5},{5... | collective-permute-start | bytes 589832 | tf_op jit(solution)/shard_map/ppermute | solution.py:26
  16.4 64.2 %collective-permute-start.2 = (f32[4,24,1,512]{3,1,2,0:T(8,128)}, f32[4,24,1,512]{3,1,2,0:T(8,128)}, u32[]{:S(2)}, u32[]{:S(2)}) collective-permute-start(f32[4,24,1,512]{3,1,2,0:T(8,128)} %get-tuple-element.155), channel_id=1, source_target_pairs={{4,0},{8,4},{12,8},{16,12},{20,16},{24,20},{28,24},{0,28},{5,1},{9... | collective-permute-start | bytes 589832 | tf_op jit(solution)/shard_map/ppermute | solution.py:28
  52.4 22.1 %copy-start.5 = (f32[12,512]{1,0:T(8,128)S(1)}, f32[12,512]{1,0:T(8,128)}, u32[]{:S(2)}) copy-start(f32[12,512]{1,0:T(8,128)} %copy-done.4) | copy-start | bytes 73732
  52.4 22.1 %copy-start.7 = (f32[12,512]{1,0:T(8,128)S(1)}, f32[12,512]{1,0:T(8,128)}, u32[]{:S(2)}) copy-start(f32[12,512]{1,0:T(8,128)} %copy-done.6) | copy-start | bytes 73732
  52.4 22.1 %copy-start.9 = (f32[12,512]{1,0:T(8,128)S(1)}, f32[12,512]{1,0:T(8,128)}, u32[]{:S(2)}) copy-start(f32[12,512]{1,0:T(8,128)} %copy-done.8) | copy-start | bytes 73732
  86.2 8.4 %collective-permute-start.3 = (f32[4,24,1,512]{3,1,2,0:T(8,128)S(1)}, f32[4,24,1,512]{3,1,2,0:T(8,128)S(1)}, u32[]{:S(2)}, u32[]{:S(2)}) collective-permute-start(f32[4,24,1,512]{3,1,2,0:T(8,128)S(1)} %get-tuple-element.152), channel_id=1, source_target_pairs={{0,4},{4,8},{8,12},{12,16},{16,20},{20,24},{24,28},{28,0},{1,5},{5... | collective-permute-start | bytes 589832 | tf_op jit(solution)/shard_map/ppermute | solution.py:26
  86.2 8.3 %collective-permute-start.4 = (f32[4,24,1,512]{3,1,2,0:T(8,128)S(1)}, f32[4,24,1,512]{3,1,2,0:T(8,128)S(1)}, u32[]{:S(2)}, u32[]{:S(2)}) collective-permute-start(f32[4,24,1,512]{3,1,2,0:T(8,128)S(1)} %get-tuple-element.151), channel_id=1, source_target_pairs={{4,0},{8,4},{12,8},{16,12},{20,16},{24,20},{28,24},{0,28},{5,1},{9... | collective-permute-start | bytes 589832 | tf_op jit(solution)/shard_map/ppermute | solution.py:28
  96.5 22.3 %copy-start.19 = (f32[8,512]{1,0:T(8,128)S(1)}, f32[8,512]{1,0:T(8,128)}, u32[]{:S(2)}) copy-start(f32[8,512]{1,0:T(8,128)} %slice.830) | copy-start | bytes 49156
  96.5 22.3 %copy-start.20 = (f32[8,512]{1,0:T(8,128)S(1)}, f32[8,512]{1,0:T(8,128)}, u32[]{:S(2)}) copy-start(f32[8,512]{1,0:T(8,128)} %slice.838) | copy-start | bytes 49156
  96.5 22.3 %copy-start.21 = (f32[8,512]{1,0:T(8,128)S(1)}, f32[8,512]{1,0:T(8,128)}, u32[]{:S(2)}) copy-start(f32[8,512]{1,0:T(8,128)} %slice.846) | copy-start | bytes 49156
  96.5 22.6 %copy-start.18 = (f32[8,512]{1,0:T(8,128)S(1)}, f32[8,512]{1,0:T(8,128)}, u32[]{:S(2)}) copy-start(f32[8,512]{1,0:T(8,128)} %slice.817) | copy-start | bytes 49156
  96.5 22.7 %copy-start.17 = (f32[8,512]{1,0:T(8,128)S(1)}, f32[8,512]{1,0:T(8,128)}, u32[]{:S(2)}) copy-start(f32[8,512]{1,0:T(8,128)} %slice.828) | copy-start | bytes 49156
  96.5 22.8 %copy-start.16 = (f32[8,512]{1,0:T(8,128)S(1)}, f32[8,512]{1,0:T(8,128)}, u32[]{:S(2)}) copy-start(f32[8,512]{1,0:T(8,128)} %slice.834) | copy-start | bytes 49156
  96.5 22.9 %copy-start.15 = (f32[8,512]{1,0:T(8,128)S(1)}, f32[8,512]{1,0:T(8,128)}, u32[]{:S(2)}) copy-start(f32[8,512]{1,0:T(8,128)} %slice.836) | copy-start | bytes 49156
  96.5 23.0 %copy-start.14 = (f32[8,512]{1,0:T(8,128)S(1)}, f32[8,512]{1,0:T(8,128)}, u32[]{:S(2)}) copy-start(f32[8,512]{1,0:T(8,128)} %slice.842) | copy-start | bytes 49156
  96.5 23.1 %copy-start.13 = (f32[8,512]{1,0:T(8,128)S(1)}, f32[8,512]{1,0:T(8,128)}, u32[]{:S(2)}) copy-start(f32[8,512]{1,0:T(8,128)} %slice.844) | copy-start | bytes 49156
  113.7 1.4 %collective-permute-start.5 = (f32[3,1,512]{2,0,1:T(4,128)S(1)}, f32[3,1,512]{2,0,1:T(4,128)S(1)}, u32[]{:S(2)}, u32[]{:S(2)}) collective-permute-start(f32[3,1,512]{2,0,1:T(4,128)S(1)} %get-tuple-element.169), channel_id=1, source_target_pairs={{4,0},{8,4},{12,8},{16,12},{20,16},{24,20},{28,24},{0,28},{5,1},{9... | collective-permute-start | bytes 18440 | tf_op jit(solution)/shard_map/ppermute | solution.py:28
  113.7 4.9 %collective-permute-start.6 = (f32[3,1,512]{2,0,1:T(4,128)S(1)}, f32[3,1,512]{2,0,1:T(4,128)S(1)}, u32[]{:S(2)}, u32[]{:S(2)}) collective-permute-start(f32[3,1,512]{2,0,1:T(4,128)S(1)} %get-tuple-element.170), channel_id=1, source_target_pairs={{0,4},{4,8},{8,12},{12,16},{16,20},{20,24},{24,28},{28,0},{1,5},{5... | collective-permute-start | bytes 18440 | tf_op jit(solution)/shard_map/ppermute | solution.py:26
  132.6 5.2 %collective-permute-start.7 = (f32[2,16,256]{2,0,1:T(2,128)S(1)}, f32[2,16,256]{2,0,1:T(2,128)S(1)}, u32[]{:S(2)}, u32[]{:S(2)}) collective-permute-start(f32[2,16,256]{2,0,1:T(2,128)S(1)} %pad_dynamic-slice_fusion.1), channel_id=1, source_target_pairs={{28,0},{0,4},{4,8},{8,12},{12,16},{16,20},{20,24},{24,28},{29,1},{... | collective-permute-start | bytes 98312 | tf_op jit(solution)/shard_map/ppermute | solution.py:16
  (18 other events, 53.3 us)
where the time goes:
time: 139 us; the launch traced here: 138 us
  local copies, waits for them, and re-layouts  72.9 us (52%)
  blocking collectives  26 us (19%)
  other arithmetic  17.6 us (13%)
  waiting for transfers between devices  10.8 us (8%)
  starting transfers between devices  8.79 us (6%)
  between operations  1.45 us (1%)
    slice x1, local copies, waits for them, and re-layouts, per_device(): window[:, step_row // 2:step_row // 2 + list_rows, step_row % 2, :, step_...  21.7 us
    reshape x1, local copies, waits for them, and re-layouts, per_device(): paired[:, first_row:first_row + 2 * (list_rows + 1)]  19.8 us
    psum x1, blocking collectives, per_device(): stress = lax.psum(stress, 'spec')  16 us
    all_gather x1, blocking collectives, per_device(): row_local = lax.all_gather(masked, 'spec', axis=2, tiled=True)  9.94 us
    reshape x1, local copies, waits for them, and re-layouts, per_device(): flat_grid = grid.reshape(2, 2 * (wave_rows + 1), ocean_cols)  7.66 us
    unnamed x72, local copies, waits for them, and re-layouts  7.16 us
    ppermute x3, starting transfers between devices, with_halo(): lax.ppermute(head, axis, [((i + 1) % count, i) for i in range(count)])  7.11 us
    ppermute x3, waiting for transfers between devices, with_halo(): lax.ppermute(tail, axis, [(i, (i + 1) % count) for i in range(count)])  7.02 us
  transfers between devices with their start and end apart: 8, of which 4 were waited for; matrix products, arithmetic and copies ran while one was open for 47% of the time, Pallas kernels for 0%

commit v1 on v0

--- a/solution.py
+++ b/solution.py
@@ -86,7 +86,12 @@
 def per_device(action, currents, wet, courant, energy, src, weights):
     wet_float = wet.astype(jnp.float32)
     masked = currents * wet_float[None]
-    row_local = lax.all_gather(masked, "spec", axis=2, tiled=True)
+    ring = [masked]
+    for hop in range(3):
+        ring.append(lax.ppermute(ring[-1], "spec", [(dev, (dev + 1) % 4) for dev in range(4)]))
+    row_local = jnp.roll(
+        jnp.concatenate(ring[::-1], axis=2), (lax.axis_index("spec") + 1) * ring[0].shape[2], axis=2
+    )
     row_next = from_behind(row_local, "space", -1)
     ocean_rows = row_local.shape[1]
     ocean_cols = row_local.shape[2]

time: 139 us -> 143 us (1.029)
  blocking collectives: 26 us -> 14.8 us
  waiting for transfers between devices: 10.8 us -> 17.4 us
  starting transfers between devices: 8.79 us -> 12.9 us
  local copies, waits for them, and re-layouts: 72.9 us -> 75.9 us
    all_gather x1 -> x0, blocking collectives: 9.94 us -> none  [per_device(): row_local = lax.all_gather(masked, 'spec', axis=2, tiled=True)]
    ppermute x0 -> x3, waiting for transfers between devices: none -> 6.22 us  [per_device(): lax.ppermute(ring[-1], 'spec', [(dev, (dev + 1) % 4) for dev in range(4)])]
    ppermute x0 -> x3, starting transfers between devices: none -> 5.1 us  [per_device(): lax.ppermute(ring[-1], 'spec', [(dev, (dev + 1) % 4) for dev in range(4)])]
    slice x9, local copies, waits for them, and re-layouts: 5.42 us -> 8.45 us  [per_device(): placed = tables[3 * step_row + step_col][2:2 + wave_rows][None] * force]
    unnamed x72 -> x76, local copies, waits for them, and re-layouts: 7.16 us -> 7.23 us
  transfers between devices with their start and end apart: 8 -> 11, of which waited for: 4 -> 6; matrix products, arithmetic and copies ran while one was open for 47% -> 49% of each run, Pallas kernels for 0% -> 0%
where the time goes in v1:
time: 143 us; the launch traced here: 142 us
  local copies, waits for them, and re-layouts  75.9 us (53%)
  other arithmetic  19 us (13%)
  waiting for transfers between devices  17.4 us (12%)
  blocking collectives  14.8 us (10%)
  starting transfers between devices  12.9 us (9%)
  between operations  1.52 us (1%)
    slice x1, local copies, waits for them, and re-layouts, per_device(): window[:, step_row // 2:step_row // 2 + list_rows, step_row % 2, :, step_...  21.6 us
    reshape x1, local copies, waits for them, and re-layouts, per_device(): paired[:, first_row:first_row + 2 * (list_rows + 1)]  19.9 us
    psum x1, blocking collectives, per_device(): stress = lax.psum(stress, 'spec')  14.8 us
    slice x9, local copies, waits for them, and re-layouts, per_device(): placed = tables[3 * step_row + step_col][2:2 + wave_rows][None] * force  8.45 us
    reshape x1, local copies, waits for them, and re-layouts, per_device(): flat_grid = grid.reshape(2, 2 * (wave_rows + 1), ocean_cols)  7.66 us
    ppermute x3, waiting for transfers between devices, with_halo(): lax.ppermute(tail, axis, [(i, (i + 1) % count) for i in range(count)])  7.37 us
    unnamed x76, local copies, waits for them, and re-layouts  7.23 us
    ppermute x3, starting transfers between devices, with_halo(): lax.ppermute(head, axis, [((i + 1) % count, i) for i in range(count)])  6.64 us
  transfers between devices with their start and end apart: 11, of which 6 were waited for; matrix products, arithmetic and copies ran while one was open for 49% of the time, Pallas kernels for 0%

profile of v1, /device:TPU:0, one launch (start us, length us, event | category | flops | bytes accessed | tf_op | source)
XLA Modules:
  0.0 142.3 jit_solution(10562811540553478179)
XLA Ops:
  2.2 3.0 %collective-permute-start = (f32[2,16,256]{2,0,1:T(2,128)S(1)}, f32[2,16,256]{2,0,1:T(2,128)S(1)}, u32[]{:S(2)}, u32[]{:S(2)}) collective-permute-start(f32[2,16,256]{2,0,1:T(2,128)S(1)} %copy_multiply_fusion), channel_id=1, source_target_pairs={{0,1},{1,2},{2,3},{3,0},{4,5},{5,6},{6,7},{7,4},{8,9},{9,10},{10,1... | collective-permute-start | bytes 98312 | tf_op jit(solution)/shard_map/ppermute | solution.py:91
  5.2 2.3 %copy.134 = f32[4,24,8,512]{3,1,2,0:T(8,128)S(1)} copy(f32[4,24,8,512]{3,2,1,0:T(8,128)} %param.25) | data formatting | bytes 3145728 | tf_op args[0]
  8.3 3.5 %collective-permute-start.5 = (f32[4,24,1,512]{3,1,2,0:T(8,128)}, f32[4,24,1,512]{3,1,2,0:T(8,128)}, u32[]{:S(2)}, u32[]{:S(2)}) collective-permute-start(f32[4,24,1,512]{3,1,2,0:T(8,128)} %get-tuple-element.155), channel_id=1, source_target_pairs={{4,0},{8,4},{12,8},{16,12},{20,16},{24,20},{28,24},{0,28},{5,1},{9... | collective-permute-start | bytes 589832 | tf_op jit(solution)/shard_map/ppermute | solution.py:28
  13.4 1.5 %collective-permute-start.1 = (f32[2,16,256]{2,0,1:T(2,128)S(1)}, f32[2,16,256]{2,0,1:T(2,128)S(1)}, u32[]{:S(2)}, u32[]{:S(2)}) collective-permute-start(f32[2,16,256]{2,0,1:T(2,128)S(1)} %collective-permute-done), channel_id=1, source_target_pairs={{0,1},{1,2},{2,3},{3,0},{4,5},{5,6},{6,7},{7,4},{8,9},{9,10},{10,1... | collective-permute-start | bytes 98312 | tf_op jit(solution)/shard_map/ppermute | solution.py:91
  15.5 2.7 %collective-permute-done.1 = f32[2,16,256]{2,0,1:T(2,128)S(1)} collective-permute-done((f32[2,16,256]{2,0,1:T(2,128)S(1)}, f32[2,16,256]{2,0,1:T(2,128)S(1)}, u32[]{:S(2)}, u32[]{:S(2)}) %collective-permute-start.1) | collective-permute-done | bytes 32800 | tf_op jit(solution)/shard_map/ppermute | solution.py:91
  19.4 3.6 %collective-permute-done.2 = f32[2,16,256]{2,0,1:T(2,128)S(1)} collective-permute-done((f32[2,16,256]{2,0,1:T(2,128)S(1)}, f32[2,16,256]{2,0,1:T(2,128)S(1)}, u32[]{:S(2)}, u32[]{:S(2)}) %collective-permute-start.2) | collective-permute-done | bytes 32800 | tf_op jit(solution)/shard_map/ppermute | solution.py:91
  25.1 1.4 %slice.802 = f32[4,23,8,512]{3,1,2,0:T(8,128)} slice(f32[4,24,8,512]{3,1,2,0:T(8,128)S(1)} %copy.134), slice={[0:4], [1:24], [0:8], [0:512]} | slice | bytes 3014656 | tf_op jit(solution)/shard_map/jit(_roll_static)/slice | solution.py:61
  29.0 1.4 slice.828
  30.4 1.4 slice.834
  33.7 1.4 slice.844
  37.3 19.9 %reshape.996 = f32[2,13,2,512,2]{4,3,0,2,1:T(8,128)} reshape(f32[2,26,1024]{2,0,1:T(2,128)S(1)} %pad_maximum_fusion) | data formatting | bytes 425984 | tf_op jit(solution)/shard_map/reshape | solution.py:104
  57.2 21.6 %slice_reduce_fusion.4 = (f32[2,12,512]{2,0,1:T(2,128)S(1)}, f32[2,12,512]{2,0,1:T(2,128)S(1)}, f32[2,12,512]{2,0,1:T(2,128)S(1)}, f32[2,12,512]{2,0,1:T(2,128)S...) fusion(f32[2,13,2,512,2]{4,3,0,2,1:T(8,128)} %reshape.996), kind=kLoop, calls=%fused_computation.4 | loop fusion | bytes 589824 | tf_op jit(solution)/shard_map/slice | solution.py:110
  82.8 1.9 %fusion.8 = (f32[4,24,8,512]{3,1,2,0:T(8,128)S(1)}, f32[4,24,8,512]{3,1,2,0:T(8,128)S(1)}) fusion(f32[4,1,8,512]{3,1,2,0:T(1,128)S(1)} %copy.144, f32[4,23,8,512]{3,1,2,0:T(8,128)S(1)} %copy-done.3, f32[24,8,512]{2,0,1:T(8,128)S(1)} %maximum_minimum_fusion.1, f32[24,8,512]{2,0,1:T(8,128)S(1)} %get-tuple-element.171, f32[4,24,8,512]{3,2,1,0:T(8,128)S(1)} %copy-done.2, ...), kind=kLoop, calls=%fused_computation.26 | loop fusion | flops 4718592 | bytes 10240384 | tf_op jit(solution)/shard_map/add | solution.py:59
  86.1 1.5 %fusion = f32[4,24,9,512]{3,1,2,0:T(8,128)S(1)} fusion(f32[4,24,8,512]{3,1,2,0:T(8,128)S(1)} %copy-done.1, f32[4,24,1,512]{3,1,2,0:T(8,128)} %collective-permute-done.4, f32[4,24,1,512]{3,1,2,0:T(8,128)} %collective-permute-done.5, f32[4,24,10,512]{3,1,2,0:T(8,128)S(1)} %broadcast_add_fusion), kind=kLoop, calls=%fused_computation.9 | loop fusion | flops 3096576 | bytes 7274496 | tf_op jit(solution)/shard_map/add | solution.py:56
  87.6 2.4 %fusion.5 = f32[4,24,8,512]{3,1,2,0:T(8,128)S(1)} fusion(f32[4,24,9,512]{3,1,2,0:T(8,128)S(1)} %fusion, f32[4,24,8,512]{3,1,2,0:T(8,128)S(1)} %get-tuple-element.154, f32[4,24,8,511]{3,1,2,0:T(8,128)S(1)} %bitcast.61, f32[4,24,8,1]{3,1,2,0:T(8,128)S(1)} %slice.778, f32[4,24,8,512]{3,1,2,0:T(8,128)S(1)} %get-tuple-element.153, ...), kind=kLoop, calls=%fused_computation.19 | loop fusion | flops 3145728 | bytes 12582912 | tf_op jit(solution)/shard_map/sub | solution.py:63
  91.5 3.1 %collective-permute-start.7 = (f32[4,24,1,512]{3,1,2,0:T(8,128)S(1)}, f32[4,24,1,512]{3,1,2,0:T(8,128)S(1)}, u32[]{:S(2)}, u32[]{:S(2)}) collective-permute-start(f32[4,24,1,512]{3,1,2,0:T(8,128)S(1)} %get-tuple-element.151), channel_id=1, source_target_pairs={{4,0},{8,4},{12,8},{16,12},{20,16},{24,20},{28,24},{0,28},{5,1},{9... | collective-permute-start | bytes 589832 | tf_op jit(solution)/shard_map/ppermute | solution.py:28
  95.9 3.8 %collective-permute-done.6 = f32[4,24,1,512]{3,1,2,0:T(8,128)S(1)} collective-permute-done((f32[4,24,1,512]{3,1,2,0:T(8,128)S(1)}, f32[4,24,1,512]{3,1,2,0:T(8,128)S(1)}, u32[]{:S(2)}, u32[]{:S(2)}) %collective-permute-start.6) | collective-permute-done | bytes 196640 | tf_op jit(solution)/shard_map/ppermute | solution.py:26
  100.2 1.4 %fusion.3 = f32[4,24,8,512]{3,1,2,0:T(8,128)S(1)} fusion(f32[4,24,9,512]{3,1,2,0:T(8,128)S(1)} %fusion.1, f32[4,24,8,512]{3,1,2,0:T(8,128)S(1)} %fusion.5, f32[4,24,8,512]{3,1,2,0:T(8,128)S(1)} %get-tuple-element.150, f32[4,24,8,511]{3,1,2,0:T(8,128)S(1)} %bitcast.60, f32[4,24,8,1]{3,1,2,0:T(8,128)S(1)} %slice.807, ...), kind=kLoop, calls=%fused_computation.16 | loop fusion | flops 3145728 | bytes 12582912 | tf_op jit(solution)/shard_map/sub | solution.py:63
  102.6 14.8 %psum.7 = f32[3,8,512]{2,0,1:T(4,128)S(1)} all-reduce(f32[3,8,512]{2,0,1:T(4,128)S(1)} %convolution_bitcast_fusion), channel_id=1, replica_groups=mesh['space'=8,'spec'=4] {'spec'}, use_global_device_ids=true, to_apply=%region_9.10 | all-reduce | flops 12288 | bytes 98304 | tf_op jit(solution)/shard_map/psum | solution.py:139
  119.0 3.6 %collective-permute-done.9 = f32[3,1,512]{2,0,1:T(4,128)S(1)} collective-permute-done((f32[3,1,512]{2,0,1:T(4,128)S(1)}, f32[3,1,512]{2,0,1:T(4,128)S(1)}, u32[]{:S(2)}, u32[]{:S(2)}) %collective-permute-start.9) | collective-permute-done | bytes 6176 | tf_op jit(solution)/shard_map/ppermute | solution.py:26
  123.7 5.0 %copy.148 = f32[2,9,2,512,2]{4,3,0,2,1:T(8,128)} copy(f32[2,9,2,512,2]{3,0,1,4,2:T(2,128)S(1)} %fusion.26) | data formatting | bytes 294912 | tf_op jit(solution)/shard_map/scatter-add | solution.py:153
  128.8 7.7 %reshape.1000 = f32[2,18,1024]{2,0,1:T(2,128)S(1)} reshape(f32[2,9,2,512,2]{4,3,0,2,1:T(8,128)} %copy.148) | data formatting | bytes 294912 | tf_op jit(solution)/shard_map/reshape | solution.py:154
  136.5 2.1 %copy.149 = f32[4,24,8,512]{3,2,1,0:T(8,128)} copy(f32[4,24,8,512]{3,1,2,0:T(8,128)S(1)} %fusion.3) | data formatting | bytes 3145728
  138.6 3.1 %collective-permute-done.10 = f32[2,16,256]{2,0,1:T(2,128)S(1)} collective-permute-done((f32[2,16,256]{2,0,1:T(2,128)S(1)}, f32[2,16,256]{2,0,1:T(2,128)S(1)}, u32[]{:S(2)}, u32[]{:S(2)}) %collective-permute-start.10) | collective-permute-done | bytes 32800 | tf_op jit(solution)/shard_map/ppermute | solution.py:16
  (180 shorter events, 26.9 us)
Async XLA Ops:
  2.2 11.2 %collective-permute-start = (f32[2,16,256]{2,0,1:T(2,128)S(1)}, f32[2,16,256]{2,0,1:T(2,128)S(1)}, u32[]{:S(2)}, u32[]{:S(2)}) collective-permute-start(f32[2,16,256]{2,0,1:T(2,128)S(1)} %copy_multiply_fusion), channel_id=1, source_target_pairs={{0,1},{1,2},{2,3},{3,0},{4,5},{5,6},{6,7},{7,4},{8,9},{9,10},{10,1... | collective-permute-start | bytes 98312 | tf_op jit(solution)/shard_map/ppermute | solution.py:91
  8.3 77.0 %collective-permute-start.4 = (f32[4,24,1,512]{3,1,2,0:T(8,128)}, f32[4,24,1,512]{3,1,2,0:T(8,128)}, u32[]{:S(2)}, u32[]{:S(2)}) collective-permute-start(f32[4,24,1,512]{3,1,2,0:T(8,128)} %get-tuple-element.156), channel_id=1, source_target_pairs={{0,4},{4,8},{8,12},{12,16},{16,20},{20,24},{24,28},{28,0},{1,5},{5... | collective-permute-start | bytes 589832 | tf_op jit(solution)/shard_map/ppermute | solution.py:26
  8.3 77.0 %collective-permute-start.5 = (f32[4,24,1,512]{3,1,2,0:T(8,128)}, f32[4,24,1,512]{3,1,2,0:T(8,128)}, u32[]{:S(2)}, u32[]{:S(2)}) collective-permute-start(f32[4,24,1,512]{3,1,2,0:T(8,128)} %get-tuple-element.155), channel_id=1, source_target_pairs={{4,0},{8,4},{12,8},{16,12},{20,16},{24,20},{28,24},{0,28},{5,1},{9... | collective-permute-start | bytes 589832 | tf_op jit(solution)/shard_map/ppermute | solution.py:28
  13.4 4.8 %collective-permute-start.1 = (f32[2,16,256]{2,0,1:T(2,128)S(1)}, f32[2,16,256]{2,0,1:T(2,128)S(1)}, u32[]{:S(2)}, u32[]{:S(2)}) collective-permute-start(f32[2,16,256]{2,0,1:T(2,128)S(1)} %collective-permute-done), channel_id=1, source_target_pairs={{0,1},{1,2},{2,3},{3,0},{4,5},{5,6},{6,7},{7,4},{8,9},{9,10},{10,1... | collective-permute-start | bytes 98312 | tf_op jit(solution)/shard_map/ppermute | solution.py:91
  18.2 4.8 %collective-permute-start.2 = (f32[2,16,256]{2,0,1:T(2,128)S(1)}, f32[2,16,256]{2,0,1:T(2,128)S(1)}, u32[]{:S(2)}, u32[]{:S(2)}) collective-permute-start(f32[2,16,256]{2,0,1:T(2,128)S(1)} %collective-permute-done.1), channel_id=1, source_target_pairs={{0,1},{1,2},{2,3},{3,0},{4,5},{5,6},{6,7},{7,4},{8,9},{9,10},{10,1... | collective-permute-start | bytes 98312 | tf_op jit(solution)/shard_map/ppermute | solution.py:91
  23.2 13.1 %collective-permute-start.3 = (f32[2,16,1024]{2,0,1:T(2,128)S(1)}, f32[2,16,1024]{2,0,1:T(2,128)}, u32[]{:S(2)}, u32[]{:S(2)}) collective-permute-start(f32[2,16,1024]{2,0,1:T(2,128)S(1)} %constant_dynamic-slice_fusion), channel_id=1, source_target_pairs={{4,0},{8,4},{12,8},{16,12},{20,16},{24,20},{28,24},{0,28},{5,1},{9... | collective-permute-start | bytes 393224 | tf_op jit(solution)/shard_map/ppermute | solution.py:16
  57.2 22.1 %copy-start.5 = (f32[12,512]{1,0:T(8,128)S(1)}, f32[12,512]{1,0:T(8,128)}, u32[]{:S(2)}) copy-start(f32[12,512]{1,0:T(8,128)} %get-tuple-element.139) | copy-start | bytes 73732
  57.2 22.1 %copy-start.6 = (f32[12,512]{1,0:T(8,128)S(1)}, f32[12,512]{1,0:T(8,128)}, u32[]{:S(2)}) copy-start(f32[12,512]{1,0:T(8,128)} %get-tuple-element.140) | copy-start | bytes 73732
  57.2 22.1 %copy-start.7 = (f32[12,512]{1,0:T(8,128)S(1)}, f32[12,512]{1,0:T(8,128)}, u32[]{:S(2)}) copy-start(f32[12,512]{1,0:T(8,128)} %get-tuple-element.141) | copy-start | bytes 73732
  57.2 22.1 %copy-start.8 = (f32[12,512]{1,0:T(8,128)S(1)}, f32[12,512]{1,0:T(8,128)}, u32[]{:S(2)}) copy-start(f32[12,512]{1,0:T(8,128)} %get-tuple-element.142) | copy-start | bytes 73732
  90.9 8.7 %collective-permute-start.6 = (f32[4,24,1,512]{3,1,2,0:T(8,128)S(1)}, f32[4,24,1,512]{3,1,2,0:T(8,128)S(1)}, u32[]{:S(2)}, u32[]{:S(2)}) collective-permute-start(f32[4,24,1,512]{3,1,2,0:T(8,128)S(1)} %get-tuple-element.152), channel_id=1, source_target_pairs={{0,4},{4,8},{8,12},{12,16},{16,20},{20,24},{24,28},{28,0},{1,5},{5... | collective-permute-start | bytes 589832 | tf_op jit(solution)/shard_map/ppermute | solution.py:26
  91.5 8.2 %collective-permute-start.7 = (f32[4,24,1,512]{3,1,2,0:T(8,128)S(1)}, f32[4,24,1,512]{3,1,2,0:T(8,128)S(1)}, u32[]{:S(2)}, u32[]{:S(2)}) collective-permute-start(f32[4,24,1,512]{3,1,2,0:T(8,128)S(1)} %get-tuple-element.151), channel_id=1, source_target_pairs={{4,0},{8,4},{12,8},{16,12},{20,16},{24,20},{28,24},{0,28},{5,1},{9... | collective-permute-start | bytes 589832 | tf_op jit(solution)/shard_map/ppermute | solution.py:28
  101.6 21.0 %copy-start.17 = (f32[8,512]{1,0:T(8,128)S(1)}, f32[8,512]{1,0:T(8,128)}, u32[]{:S(2)}) copy-start(f32[8,512]{1,0:T(8,128)} %slice.830) | copy-start | bytes 49156
  101.6 21.0 %copy-start.18 = (f32[8,512]{1,0:T(8,128)S(1)}, f32[8,512]{1,0:T(8,128)}, u32[]{:S(2)}) copy-start(f32[8,512]{1,0:T(8,128)} %slice.838) | copy-start | bytes 49156
  101.7 21.0 %copy-start.19 = (f32[8,512]{1,0:T(8,128)S(1)}, f32[8,512]{1,0:T(8,128)}, u32[]{:S(2)}) copy-start(f32[8,512]{1,0:T(8,128)} %slice.846) | copy-start | bytes 49156
  101.7 21.3 %copy-start.16 = (f32[8,512]{1,0:T(8,128)S(1)}, f32[8,512]{1,0:T(8,128)}, u32[]{:S(2)}) copy-start(f32[8,512]{1,0:T(8,128)} %slice.817) | copy-start | bytes 49156
  101.7 21.4 %copy-start.15 = (f32[8,512]{1,0:T(8,128)S(1)}, f32[8,512]{1,0:T(8,128)}, u32[]{:S(2)}) copy-start(f32[8,512]{1,0:T(8,128)} %slice.828) | copy-start | bytes 49156
  101.7 21.5 %copy-start.14 = (f32[8,512]{1,0:T(8,128)S(1)}, f32[8,512]{1,0:T(8,128)}, u32[]{:S(2)}) copy-start(f32[8,512]{1,0:T(8,128)} %slice.834) | copy-start | bytes 49156
  101.7 21.6 %copy-start.13 = (f32[8,512]{1,0:T(8,128)S(1)}, f32[8,512]{1,0:T(8,128)}, u32[]{:S(2)}) copy-start(f32[8,512]{1,0:T(8,128)} %slice.836) | copy-start | bytes 49156
  101.7 21.8 %copy-start.12 = (f32[8,512]{1,0:T(8,128)S(1)}, f32[8,512]{1,0:T(8,128)}, u32[]{:S(2)}) copy-start(f32[8,512]{1,0:T(8,128)} %slice.842) | copy-start | bytes 49156
  101.7 21.8 %copy-start.11 = (f32[8,512]{1,0:T(8,128)S(1)}, f32[8,512]{1,0:T(8,128)}, u32[]{:S(2)}) copy-start(f32[8,512]{1,0:T(8,128)} %slice.844) | copy-start | bytes 49156
  117.6 1.4 collective-permute-start.8
  117.6 4.9 %collective-permute-start.9 = (f32[3,1,512]{2,0,1:T(4,128)S(1)}, f32[3,1,512]{2,0,1:T(4,128)S(1)}, u32[]{:S(2)}, u32[]{:S(2)}) collective-permute-start(f32[3,1,512]{2,0,1:T(4,128)S(1)} %get-tuple-element.170), channel_id=1, source_target_pairs={{0,4},{4,8},{8,12},{12,16},{16,20},{20,24},{24,28},{28,0},{1,5},{5... | collective-permute-start | bytes 18440 | tf_op jit(solution)/shard_map/ppermute | solution.py:26
  136.5 5.2 %collective-permute-start.10 = (f32[2,16,256]{2,0,1:T(2,128)S(1)}, f32[2,16,256]{2,0,1:T(2,128)S(1)}, u32[]{:S(2)}, u32[]{:S(2)}) collective-permute-start(f32[2,16,256]{2,0,1:T(2,128)S(1)} %pad_dynamic-slice_fusion.1), channel_id=1, source_target_pairs={{28,0},{0,4},{4,8},{8,12},{12,16},{16,20},{20,24},{24,28},{29,1},{... | collective-permute-start | bytes 98312 | tf_op jit(solution)/shard_map/ppermute | solution.py:16
  (20 other events, 120.4 us)
